TPU v7x, 256 devices: a whole 4x4x8 slice. The times are simulated.
256 devices in a mesh: gx: 4 (over x), gy: 8 (over y, core), gz: 8 (over z).
Axes of the slice: x: 4, y: 4, z: 8, core: 2. Of those that a mesh axis runs over, the one named last changes fastest.
Arguments:
- right_side: float32 [64, 256, 1024], P('gx', 'gy', 'gz'), may hold values from -8 to 8
- diagonal: float32 [64, 256, 1024], P('gx', 'gy', 'gz'), may hold values from 0.16 to 6.1
Outputs:
- solution_field: float32 [64, 256, 1024], P('gx', 'gy', 'gz')
- residual: float32 [64, 256, 1024], P('gx', 'gy', 'gz')
All inputs are finite; a program needn't handle non-finite values.
Results may differ from a plain program's by a relative error of at most 0.0003.
Values sent between devices are 32-bit elements; how exact they have to be, the bound alone decides.
No kernel may reach another device: no remote copies, remote signals or barrier semaphores. Data moves between devices by JAX's collectives and lax.ppermute only.
A program may use at most 128 MiB of HBM per device.

v0:
```python
import jax
import jax.numpy as jnp
from jax import lax
from jax.sharding import Mesh
from jax.sharding import PartitionSpec as P

ITERS = 2
GX_GY_GZ = ("gx", "gy_0", "gy_1", "gz")
GY = ("gy_0", "gy_1")


def extended(cells, sides, width):
    for axis, dim in sides:
        count = lax.axis_size(axis)
        ends = count - 1
        head = lax.slice_in_dim(cells, 0, width, axis=dim)
        tail = lax.slice_in_dim(cells, cells.shape[dim] - width, cells.shape[dim], axis=dim)
        cells = jnp.concatenate(
            [
                lax.ppermute(tail, axis, [(i, (i + 1) % count) for i in range(ends)]),
                cells,
                lax.ppermute(head, axis, [((i + 1) % count, i) for i in range(ends)]),
            ],
            axis=dim,
        )
    return cells


def in_order(tiles, dim):
    tiles = jnp.moveaxis(tiles, 0, dim)
    shape = tiles.shape
    return tiles.reshape(*shape[:dim], shape[dim] * shape[dim + 1], *shape[dim + 2 :])


def one_gather(arrays, axis, dims):
    line = jnp.concatenate([a.reshape(-1) for a in arrays])
    lines, at, outs = (lax.all_gather(line, axis), 0, [])
    for a, dim in zip(arrays, dims):
        tiles = lines[:, at : at + a.size].reshape(-1, *a.shape)
        outs.append(in_order(tiles, dim))
        at += a.size
    return tuple(outs)


def over_axes(array, axes):
    for axis in axes:
        array = lax.psum(array, axis)
    return array


def box_sum(padded):
    total = padded[:-2] + padded[1:-1] + padded[2:]
    total = total[:, :-2] + total[:, 1:-1] + total[:, 2:]
    return total[:, :, :-2] + total[:, :, 1:-1] + total[:, :, 2:]


def operate(field, extra):
    padded = extended(field, (("gx", 0), (GY, 1), ("gz", 2)), 1)
    return (27.0 + extra) * field - box_sum(padded)


def operate_column(field, extra):
    padded = extended(field, (("gx", 0), (GY, 1)), 1)
    padded = jnp.pad(padded, ((0, 0), (0, 0), (1, 1)))
    return (27.0 + extra) * field - box_sum(padded)


def cheb_terms(lower):
    upper = 58.0
    theta = (upper + lower) / 2.0
    delta = (upper - lower) / 2.0
    return (theta, delta, theta / delta)


def smooth(rhs, extra, degree, lower, apply):
    theta, delta, sigma = cheb_terms(lower)
    rho = 1.0 / sigma
    step = rhs / theta
    total = step
    remain = rhs
    for count in range(degree - 1):
        remain = remain - apply(step, extra)
        rho_next = 1.0 / (2.0 * sigma - rho)
        step = rho_next * rho * step + 2.0 * rho_next / delta * remain
        total = total + step
        rho = rho_next
    return total


def blocks(field):
    a, b, c = field.shape
    return field.reshape(a // 2, 2, b // 2, 2, c // 2, 2)


def restrict(field):
    return 0.5 * blocks(field).sum(axis=(1, 3, 5))


def prolong(field):
    a, b, c = field.shape
    wide = jnp.broadcast_to(field[:, None, :, None, :, None], (a, 2, b, 2, c, 2))
    return wide.reshape(2 * a, 2 * b, 2 * c)


def inside_mask(shape):
    places = (lax.axis_index("gx"), lax.axis_index(GY), lax.axis_index("gz"))
    counts = (lax.axis_size("gx"), lax.axis_size(GY), lax.axis_size("gz"))
    result = jnp.ones((1, 1, 1), jnp.float32)
    for dim in range(3):
        count = shape[dim]
        spots = places[dim] * count + jnp.arange(count + 2, dtype=jnp.int32) - 1
        valid = ((spots >= 0) & (spots < counts[dim] * count)).astype(jnp.float32)
        dims_shape = [1, 1, 1]
        dims_shape[dim] = count + 2
        result = result * valid.reshape(dims_shape)
    return result


def deep_pre(r_zero, extra_zero, extra_wide, inside):
    theta, delta, sigma = cheb_terms(7.0)
    rho = 1.0 / sigma
    wide = extended(r_zero, (("gx", 0), (GY, 1), ("gz", 2)), 2)
    step = wide / theta
    middle = step[1:-1, 1:-1, 1:-1]
    extra_mid = extra_wide[1:-1, 1:-1, 1:-1]
    remain = (wide[1:-1, 1:-1, 1:-1] - ((27.0 + extra_mid) * middle - box_sum(step))) * inside
    rho_next = 1.0 / (2.0 * sigma - rho)
    smoothed = middle + (rho_next * rho * middle + 2.0 * rho_next / delta * remain)
    inner = smoothed[1:-1, 1:-1, 1:-1]
    rest = r_zero - ((27.0 + extra_zero) * inner - box_sum(smoothed))
    return (inner, rest)


def coarse_solve(r_two, extra_two):
    whole_r, whole_e = one_gather((r_two, extra_two), "gz", (2, 2))
    solved = smooth(whole_r, whole_e, 3, 1.0, operate_column)
    left = whole_r - operate_column(solved, whole_e)
    shift_line = jnp.sum(left, axis=2, keepdims=True) / jnp.sum(
        1.0 + whole_e, axis=2, keepdims=True
    )
    start = lax.axis_index("gz") * r_two.shape[2]
    return lax.dynamic_slice_in_dim(solved, start, r_two.shape[2], 2) + shift_line


def vcycle(r_zero, extra_zero, extra_one, extra_two, extra_wide, inside):
    z_zero, rest = deep_pre(r_zero, extra_zero, extra_wide, inside)
    r_one = restrict(rest)
    z_one = smooth(r_one, extra_one, 2, 7.0, operate)
    r_two = restrict(r_one - operate(z_one, extra_one))
    z_two = coarse_solve(r_two, extra_two)
    z_one = z_one + prolong(z_two)
    z_one = z_one + smooth(r_one - operate(z_one, extra_one), extra_one, 2, 7.0, operate)
    z_zero = z_zero + prolong(z_one)
    z_zero = z_zero + smooth(r_zero - operate(z_zero, extra_zero), extra_zero, 2, 7.0, operate)
    return z_zero


def local(right_side, diagonal):
    extra_one = blocks(diagonal).mean(axis=(1, 3, 5))
    extra_two = blocks(extra_one).mean(axis=(1, 3, 5))
    extra_wide = None
    inside = None
    extra_wide = extended(diagonal, (("gx", 0), (GY, 1), ("gz", 2)), 2)
    inside = inside_mask(diagonal.shape)
    solution_field = jnp.zeros_like(right_side)
    residual = right_side
    direction = jnp.zeros_like(right_side)
    image = jnp.zeros_like(right_side)
    rz_prev = jnp.float32(1.0)
    curve_prev = jnp.float32(0.0)
    for step in range(ITERS):
        precond = vcycle(residual, diagonal, extra_one, extra_two, extra_wide, inside)
        applied = operate(precond, diagonal)
        rz_now, zw_sum, zq_sum = (
            over_axes(jnp.sum(residual * precond), GX_GY_GZ),
            over_axes(jnp.sum(precond * applied), GX_GY_GZ),
            over_axes(jnp.sum(precond * image), GX_GY_GZ),
        )
        beta = 0.0 if step == 0 else rz_now / rz_prev
        direction = precond + beta * direction
        image = applied + beta * image
        curve = zw_sum + 2.0 * beta * zq_sum + beta * beta * curve_prev
        alpha = rz_now / curve
        solution_field = solution_field + alpha * direction
        residual = residual - alpha * image
        rz_prev = rz_now
        curve_prev = curve
    return (solution_field, residual)


def solution(mesh):
    torus = Mesh(
        mesh.devices.reshape(mesh.shape["gx"], 4, 2, mesh.shape["gz"]), ("gx", "gy_0", "gy_1", "gz")
    )
    in_specs = (P("gx", GY, "gz"), P("gx", GY, "gz"))
    out_specs = (P("gx", GY, "gz"), P("gx", GY, "gz"))
    return jax.shard_map(local, mesh=torus, in_specs=in_specs, out_specs=out_specs, check_vma=False)
```

profile of v0, /device:TPU:2, one launch (start us, length us, event | category | flops | bytes accessed | tf_op | source)
XLA Modules:
  0.0 846.8 jit_solution(9266118594562411616)
XLA Ops:
  53.9 18.1 %reshape.156 = f32[8,2,16,2,64,2]{5,4,3,2,1,0:T(8,128)} reshape(f32[16,32,128]{2,1,0:T(8,128)S(1)} %fusion.32) | data formatting | bytes 524288 | tf_op jit(solution)/shard_map/reshape | solution.py:92
  72.0 7.0 reduce_sum.158
  102.1 18.1 %reshape.157 = f32[8,2,16,2,64,2]{5,4,3,2,1,0:T(8,128)} reshape(f32[16,32,128]{2,1,0:T(8,128)S(1)} %copy-done) | data formatting | bytes 524288 | tf_op jit(solution)/shard_map/reshape | solution.py:92
  120.2 7.0 reduce_sum.159
  168.4 25.5 %all-gather = f32[16384]{0:T(1024)S(1)} all-gather(f32[2048]{0:T(1024)S(1)} %pad_maximum_fusion.41), channel_id=2, replica_groups=mesh['gx'=4,'gy_0'=4,'gy_1'=2,'gz'=8] {'gz'}, dimensions={0}, use_global_device_ids=true | all-gather | bytes 73728 | tf_op jit(solution)/shard_map/all_gather | solution.py:37
  294.8 6.6 broadcast_in_dim.11
  301.4 12.6 %reshape.162 = f32[16,32,128]{2,1,0:T(8,128)S(1)} reshape(f32[8,2,16,2,64,2]{5,4,3,2,1,0:T(8,128)} %broadcast_in_dim.11) | data formatting | bytes 524288 | tf_op jit(solution)/shard_map/reshape | solution.py:102
  333.8 6.1 collective-permute-done.52
  365.0 6.1 collective-permute-done.58
  396.3 6.1 collective-permute-done.64
  408.6 10.4 %all-reduce.11 = (f32[]{:T(128)}, f32[]{:T(128)}, f32[]{:T(128)}) all-reduce(f32[]{:T(128)} %get-tuple-element.7, f32[]{:T(128)} %get-tuple-element.6, f32[]{:T(128)} %get-tuple-element.5), channel_id=1, replica_groups=mesh['gx'=4,'gy_0'=4,'gy_1'=2,'gz'=8] {'gx'}, use_global_device_ids=true, to_apply=%region_8.9 | all-reduce | flops 3 | bytes 24 | tf_op jit(solution)/shard_map/psum | solution.py:47
  419.0 8.9 %all-reduce.9 = (f32[]{:T(128)}, f32[]{:T(128)}, f32[]{:T(128)}) all-reduce(f32[]{:T(128)} %get-tuple-element.23, f32[]{:T(128)} %get-tuple-element.24, f32[]{:T(128)} %get-tuple-element.25), channel_id=1, replica_groups=mesh['gx'=4,'gy_0'=4,'gy_1'=2,'gz'=8] {'gy_0'}, use_global_device_ids=true, to_apply=%region_9.10 | all-reduce | flops 3 | bytes 24 | tf_op jit(solution)/shard_map/psum | solution.py:47
  431.1 16.3 %all-reduce.7 = (f32[]{:T(128)}, f32[]{:T(128)}, f32[]{:T(128)}) all-reduce(f32[]{:T(128)} %get-tuple-element.29, f32[]{:T(128)} %get-tuple-element.30, f32[]{:T(128)} %get-tuple-element.31), channel_id=1, replica_groups=mesh['gx'=4,'gy_0'=4,'gy_1'=2,'gz'=8] {'gz'}, use_global_device_ids=true, to_apply=%region_11.12 | all-reduce | flops 3 | bytes 24 | tf_op jit(solution)/shard_map/psum | solution.py:47
  467.4 6.9 collective-permute-done.70
  482.7 18.1 %reshape.163 = f32[8,2,16,2,64,2]{5,4,3,2,1,0:T(8,128)} reshape(f32[16,32,128]{2,1,0:T(8,128)S(1)} %fusion.21) | data formatting | bytes 524288 | tf_op jit(solution)/shard_map/reshape | solution.py:92
  500.8 7.0 reduce_sum.169
  567.6 24.8 %all-gather.1 = f32[16384]{0:T(1024)S(1)} all-gather(f32[2048]{0:T(1024)S(1)} %pad_maximum_fusion.40), channel_id=3, replica_groups=mesh['gx'=4,'gy_0'=4,'gy_1'=2,'gz'=8] {'gz'}, dimensions={0}, use_global_device_ids=true | all-gather | bytes 73728 | tf_op jit(solution)/shard_map/all_gather | solution.py:37
  691.1 6.6 broadcast_in_dim.14
  697.7 12.6 %reshape.168 = f32[16,32,128]{2,1,0:T(8,128)S(1)} reshape(f32[8,2,16,2,64,2]{5,4,3,2,1,0:T(8,128)} %broadcast_in_dim.14) | data formatting | bytes 524288 | tf_op jit(solution)/shard_map/reshape | solution.py:102
  730.5 6.1 collective-permute-done.112
  791.6 6.1 collective-permute-done.124
  803.8 10.4 %all-reduce.10 = (f32[]{:T(128)}, f32[]{:T(128)}, f32[]{:T(128)}) all-reduce(f32[]{:T(128)} %get-tuple-element.4, f32[]{:T(128)} %get-tuple-element.3, f32[]{:T(128)} %get-tuple-element.2), channel_id=1, replica_groups=mesh['gx'=4,'gy_0'=4,'gy_1'=2,'gz'=8] {'gx'}, use_global_device_ids=true, to_apply=%region_28.29 | all-reduce | flops 3 | bytes 24 | tf_op jit(solution)/shard_map/psum | solution.py:47
  814.3 8.8 %all-reduce.8 = (f32[]{:T(128)}, f32[]{:T(128)}, f32[]{:T(128)}) all-reduce(f32[]{:T(128)} %get-tuple-element.20, f32[]{:T(128)} %get-tuple-element.21, f32[]{:T(128)} %get-tuple-element.22), channel_id=1, replica_groups=mesh['gx'=4,'gy_0'=4,'gy_1'=2,'gz'=8] {'gy_0'}, use_global_device_ids=true, to_apply=%region_29.30 | all-reduce | flops 3 | bytes 24 | tf_op jit(solution)/shard_map/psum | solution.py:47
  826.3 16.3 %all-reduce.6 = (f32[]{:T(128)}, f32[]{:T(128)}, f32[]{:T(128)}) all-reduce(f32[]{:T(128)} %get-tuple-element.26, f32[]{:T(128)} %get-tuple-element.27, f32[]{:T(128)} %get-tuple-element.28), channel_id=1, replica_groups=mesh['gx'=4,'gy_0'=4,'gy_1'=2,'gz'=8] {'gz'}, use_global_device_ids=true, to_apply=%region_31.32 | all-reduce | flops 3 | bytes 24 | tf_op jit(solution)/shard_map/psum | solution.py:47
  (516 shorter events, 565.1 us)
Async XLA Ops:
  1.5 13.9 %collective-permute-start.1 = (f32[2,32,128]{2,1,0:T(8,128)S(1)}, f32[2,32,128]{2,1,0:T(8,128)S(1)}, u32[]{:S(2)}, u32[]{:S(2)}) collective-permute-start(f32[2,32,128]{2,1,0:T(8,128)S(1)} %get-tuple-element.98), channel_id=1, source_target_pairs={{64,0},{128,64},{192,128},{65,1},{129,65},{193,129},{66,2},{130,66... | collective-permute-start | bytes 98312 | tf_op jit(solution)/shard_map/ppermute | solution.py:22
  5.7 8.7 %collective-permute-start = (f32[2,32,128]{2,1,0:T(8,128)S(1)}, f32[2,32,128]{2,1,0:T(8,128)S(1)}, u32[]{:S(2)}, u32[]{:S(2)}) collective-permute-start(f32[2,32,128]{2,1,0:T(8,128)S(1)} %get-tuple-element.99), channel_id=1, source_target_pairs={{0,64},{64,128},{128,192},{1,65},{65,129},{129,193},{2,66},{66,130... | collective-permute-start | bytes 98312 | tf_op jit(solution)/shard_map/ppermute | solution.py:20
  8.4 13.3 %collective-permute-start.7 = (f32[2,32,128]{2,1,0:T(8,128)S(1)}, f32[2,32,128]{2,1,0:T(8,128)S(1)}, u32[]{:S(2)}, u32[]{:S(2)}) collective-permute-start(f32[2,32,128]{2,1,0:T(8,128)S(1)} %get-tuple-element.96), channel_id=1, source_target_pairs={{64,0},{128,64},{192,128},{65,1},{129,65},{193,129},{66,2},{130,66... | collective-permute-start | bytes 98312 | tf_op jit(solution)/shard_map/ppermute | solution.py:22
  21.7 9.8 %collective-permute-start.8 = (f32[20,2,128]{2,1,0:T(2,128)S(1)}, f32[20,2,128]{2,1,0:T(2,128)S(1)}, u32[]{:S(2)}, u32[]{:S(2)}) collective-permute-start(f32[20,2,128]{2,1,0:T(2,128)S(1)} %get-tuple-element.66), channel_id=1, source_target_pairs={{0,8},{8,16},{16,24},{24,32},{32,40},{40,48},{48,56},{1,9},{9,17},... | collective-permute-start | bytes 61448 | tf_op jit(solution)/shard_map/ppermute | solution.py:20
  26.4 12.2 %collective-permute-start.4 = (f32[20,36,2]{2,1,0:T(8,128)S(1)}, f32[20,36,2]{2,1,0:T(8,128)S(1)}, u32[]{:S(2)}, u32[]{:S(2)}) collective-permute-start(f32[20,36,2]{2,1,0:T(8,128)S(1)} %get-tuple-element.50), channel_id=1, source_target_pairs={{0,1},{1,2},{2,3},{3,4},{4,5},{5,6},{6,7},{8,9},{9,10},{10,11},{11... | collective-permute-start | bytes 17288 | tf_op jit(solution)/shard_map/ppermute | solution.py:20
  30.3 12.9 %collective-permute-start.5 = (f32[20,36,2]{2,1,0:T(8,128)S(1)}, f32[20,36,2]{2,1,0:T(8,128)S(1)}, u32[]{:S(2)}, u32[]{:S(2)}) collective-permute-start(f32[20,36,2]{2,1,0:T(8,128)S(1)} %get-tuple-element.51), channel_id=1, source_target_pairs={{1,0},{2,1},{3,2},{4,3},{5,4},{6,5},{7,6},{9,8},{10,9},{11,10},{12... | collective-permute-start | bytes 17288 | tf_op jit(solution)/shard_map/ppermute | solution.py:22
  31.9 15.6 %collective-permute-start.10 = (f32[20,36,2]{2,1,0:T(8,128)S(1)}, f32[20,36,2]{2,1,0:T(8,128)S(1)}, u32[]{:S(2)}, u32[]{:S(2)}) collective-permute-start(f32[20,36,2]{2,1,0:T(8,128)S(1)} %get-tuple-element.48), channel_id=1, source_target_pairs={{0,1},{1,2},{2,3},{3,4},{4,5},{5,6},{6,7},{8,9},{9,10},{10,11},{11... | collective-permute-start | bytes 17288 | tf_op jit(solution)/shard_map/ppermute | solution.py:20
  36.4 15.5 %collective-permute-start.11 = (f32[20,36,2]{2,1,0:T(8,128)S(1)}, f32[20,36,2]{2,1,0:T(8,128)S(1)}, u32[]{:S(2)}, u32[]{:S(2)}) collective-permute-start(f32[20,36,2]{2,1,0:T(8,128)S(1)} %get-tuple-element.49), channel_id=1, source_target_pairs={{1,0},{2,1},{3,2},{4,3},{5,4},{6,5},{7,6},{9,8},{10,9},{11,10},{12... | collective-permute-start | bytes 17288 | tf_op jit(solution)/shard_map/ppermute | solution.py:22
  97.0 30.3 %collective-permute-start.16 = (f32[10,18,1]{2,1,0:T(8,128)S(1)}, f32[10,18,1]{2,1,0:T(8,128)S(1)}, u32[]{:S(2)}, u32[]{:S(2)}) collective-permute-start(f32[10,18,1]{2,1,0:T(8,128)S(1)} %get-tuple-element.114), channel_id=1, source_target_pairs={{0,1},{1,2},{2,3},{3,4},{4,5},{5,6},{6,7},{8,9},{9,10},{10,11},{11... | collective-permute-start | bytes 2168 | tf_op jit(solution)/shard_map/ppermute | solution.py:20
  100.8 26.4 %collective-permute-start.17 = (f32[10,18,1]{2,1,0:T(8,128)S(1)}, f32[10,18,1]{2,1,0:T(8,128)S(1)}, u32[]{:S(2)}, u32[]{:S(2)}) collective-permute-start(f32[10,18,1]{2,1,0:T(8,128)S(1)} %get-tuple-element.115), channel_id=1, source_target_pairs={{1,0},{2,1},{3,2},{4,3},{5,4},{6,5},{7,6},{9,8},{10,9},{11,10},{12... | collective-permute-start | bytes 2168 | tf_op jit(solution)/shard_map/ppermute | solution.py:22
  328.8 11.1 %collective-permute-start.52 = (f32[18,34,1]{2,1,0:T(8,128)S(1)}, f32[18,34,1]{2,1,0:T(8,128)S(1)}, u32[]{:S(2)}, u32[]{:S(2)}) collective-permute-start(f32[18,34,1]{2,1,0:T(8,128)S(1)} %get-tuple-element.62), channel_id=1, source_target_pairs={{0,1},{1,2},{2,3},{3,4},{4,5},{5,6},{6,7},{8,9},{9,10},{10,11},{11... | collective-permute-start | bytes 7352 | tf_op jit(solution)/shard_map/ppermute | solution.py:20
  332.5 12.2 %collective-permute-start.53 = (f32[18,34,1]{2,1,0:T(8,128)S(1)}, f32[18,34,1]{2,1,0:T(8,128)S(1)}, u32[]{:S(2)}, u32[]{:S(2)}) collective-permute-start(f32[18,34,1]{2,1,0:T(8,128)S(1)} %get-tuple-element.63), channel_id=1, source_target_pairs={{1,0},{2,1},{3,2},{4,3},{5,4},{6,5},{7,6},{9,8},{10,9},{11,10},{12... | collective-permute-start | bytes 7352 | tf_op jit(solution)/shard_map/ppermute | solution.py:22
  360.3 10.9 %collective-permute-start.58 = (f32[18,34,1]{2,1,0:T(8,128)S(1)}, f32[18,34,1]{2,1,0:T(8,128)S(1)}, u32[]{:S(2)}, u32[]{:S(2)}) collective-permute-start(f32[18,34,1]{2,1,0:T(8,128)S(1)} %get-tuple-element.60), channel_id=1, source_target_pairs={{0,1},{1,2},{2,3},{3,4},{4,5},{5,6},{6,7},{8,9},{9,10},{10,11},{11... | collective-permute-start | bytes 7352 | tf_op jit(solution)/shard_map/ppermute | solution.py:20
  363.7 12.2 %collective-permute-start.59 = (f32[18,34,1]{2,1,0:T(8,128)S(1)}, f32[18,34,1]{2,1,0:T(8,128)S(1)}, u32[]{:S(2)}, u32[]{:S(2)}) collective-permute-start(f32[18,34,1]{2,1,0:T(8,128)S(1)} %get-tuple-element.61), channel_id=1, source_target_pairs={{1,0},{2,1},{3,2},{4,3},{5,4},{6,5},{7,6},{9,8},{10,9},{11,10},{12... | collective-permute-start | bytes 7352 | tf_op jit(solution)/shard_map/ppermute | solution.py:22
  391.3 11.1 %collective-permute-start.64 = (f32[18,34,1]{2,1,0:T(8,128)S(1)}, f32[18,34,1]{2,1,0:T(8,128)S(1)}, u32[]{:S(2)}, u32[]{:S(2)}) collective-permute-start(f32[18,34,1]{2,1,0:T(8,128)S(1)} %get-tuple-element.58), channel_id=1, source_target_pairs={{0,1},{1,2},{2,3},{3,4},{4,5},{5,6},{6,7},{8,9},{9,10},{10,11},{11... | collective-permute-start | bytes 7352 | tf_op jit(solution)/shard_map/ppermute | solution.py:20
  395.0 12.2 %collective-permute-start.65 = (f32[18,34,1]{2,1,0:T(8,128)S(1)}, f32[18,34,1]{2,1,0:T(8,128)S(1)}, u32[]{:S(2)}, u32[]{:S(2)}) collective-permute-start(f32[18,34,1]{2,1,0:T(8,128)S(1)} %get-tuple-element.59), channel_id=1, source_target_pairs={{1,0},{2,1},{3,2},{4,3},{5,4},{6,5},{7,6},{9,8},{10,9},{11,10},{12... | collective-permute-start | bytes 7352 | tf_op jit(solution)/shard_map/ppermute | solution.py:22
  463.6 10.7 %collective-permute-start.70 = (f32[20,36,2]{2,1,0:T(8,128)S(1)}, f32[20,36,2]{2,1,0:T(8,128)S(1)}, u32[]{:S(2)}, u32[]{:S(2)}) collective-permute-start(f32[20,36,2]{2,1,0:T(8,128)S(1)} %get-tuple-element.46), channel_id=1, source_target_pairs={{0,1},{1,2},{2,3},{3,4},{4,5},{5,6},{6,7},{8,9},{9,10},{10,11},{11... | collective-permute-start | bytes 17288 | tf_op jit(solution)/shard_map/ppermute | solution.py:20
  466.1 12.9 %collective-permute-start.71 = (f32[20,36,2]{2,1,0:T(8,128)S(1)}, f32[20,36,2]{2,1,0:T(8,128)S(1)}, u32[]{:S(2)}, u32[]{:S(2)}) collective-permute-start(f32[20,36,2]{2,1,0:T(8,128)S(1)} %get-tuple-element.47), channel_id=1, source_target_pairs={{1,0},{2,1},{3,2},{4,3},{5,4},{6,5},{7,6},{9,8},{10,9},{11,10},{12... | collective-permute-start | bytes 17288 | tf_op jit(solution)/shard_map/ppermute | solution.py:22
  725.2 11.4 %collective-permute-start.112 = (f32[18,34,1]{2,1,0:T(8,128)S(1)}, f32[18,34,1]{2,1,0:T(8,128)S(1)}, u32[]{:S(2)}, u32[]{:S(2)}) collective-permute-start(f32[18,34,1]{2,1,0:T(8,128)S(1)} %get-tuple-element.56), channel_id=1, source_target_pairs={{0,1},{1,2},{2,3},{3,4},{4,5},{5,6},{6,7},{8,9},{9,10},{10,11},{11... | collective-permute-start | bytes 7352 | tf_op jit(solution)/shard_map/ppermute | solution.py:20
  729.2 11.9 %collective-permute-start.113 = (f32[18,34,1]{2,1,0:T(8,128)S(1)}, f32[18,34,1]{2,1,0:T(8,128)S(1)}, u32[]{:S(2)}, u32[]{:S(2)}) collective-permute-start(f32[18,34,1]{2,1,0:T(8,128)S(1)} %get-tuple-element.57), channel_id=1, source_target_pairs={{1,0},{2,1},{3,2},{4,3},{5,4},{6,5},{7,6},{9,8},{10,9},{11,10},{12... | collective-permute-start | bytes 7352 | tf_op jit(solution)/shard_map/ppermute | solution.py:22
  756.8 11.1 %collective-permute-start.118 = (f32[18,34,1]{2,1,0:T(8,128)S(1)}, f32[18,34,1]{2,1,0:T(8,128)S(1)}, u32[]{:S(2)}, u32[]{:S(2)}) collective-permute-start(f32[18,34,1]{2,1,0:T(8,128)S(1)} %get-tuple-element.54), channel_id=1, source_target_pairs={{0,1},{1,2},{2,3},{3,4},{4,5},{5,6},{6,7},{8,9},{9,10},{10,11},{11... | collective-permute-start | bytes 7352 | tf_op jit(solution)/shard_map/ppermute | solution.py:20
  760.5 12.2 %collective-permute-start.119 = (f32[18,34,1]{2,1,0:T(8,128)S(1)}, f32[18,34,1]{2,1,0:T(8,128)S(1)}, u32[]{:S(2)}, u32[]{:S(2)}) collective-permute-start(f32[18,34,1]{2,1,0:T(8,128)S(1)} %get-tuple-element.55), channel_id=1, source_target_pairs={{1,0},{2,1},{3,2},{4,3},{5,4},{6,5},{7,6},{9,8},{10,9},{11,10},{12... | collective-permute-start | bytes 7352 | tf_op jit(solution)/shard_map/ppermute | solution.py:22
  787.1 10.6 %collective-permute-start.124 = (f32[18,34,1]{2,1,0:T(8,128)S(1)}, f32[18,34,1]{2,1,0:T(8,128)S(1)}, u32[]{:S(2)}, u32[]{:S(2)}) collective-permute-start(f32[18,34,1]{2,1,0:T(8,128)S(1)} %get-tuple-element.52), channel_id=1, source_target_pairs={{0,1},{1,2},{2,3},{3,4},{4,5},{5,6},{6,7},{8,9},{9,10},{10,11},{11... | collective-permute-start | bytes 7352 | tf_op jit(solution)/shard_map/ppermute | solution.py:20
  790.3 12.2 %collective-permute-start.125 = (f32[18,34,1]{2,1,0:T(8,128)S(1)}, f32[18,34,1]{2,1,0:T(8,128)S(1)}, u32[]{:S(2)}, u32[]{:S(2)}) collective-permute-start(f32[18,34,1]{2,1,0:T(8,128)S(1)} %get-tuple-element.53), channel_id=1, source_target_pairs={{1,0},{2,1},{3,2},{4,3},{5,4},{6,5},{7,6},{9,8},{10,9},{11,10},{12... | collective-permute-start | bytes 7352 | tf_op jit(solution)/shard_map/ppermute | solution.py:22
  (118 other events, 1636.5 us)
where the time goes:
time: 859 us; the launch traced here: 847 us
  starting transfers between devices  302 us (35%)
  waiting for transfers between devices  243 us (28%)
  blocking collectives  128 us (15%)
  local copies, waits for them, and re-layouts  118 us (14%)
  other arithmetic  47 us (5%)
  between operations  8.84 us (1%)
    ppermute x63, waiting for transfers between devices, extended(): lax.ppermute(head, axis, [((i + 1) % count, i) for i in range(ends)])  184 us
    ppermute x63, starting transfers between devices, extended(): lax.ppermute(tail, axis, [(i, (i + 1) % count) for i in range(ends)])  164 us
    ppermute x63, starting transfers between devices, extended(): lax.ppermute(head, axis, [((i + 1) % count, i) for i in range(ends)])  138 us
    psum x8, blocking collectives, over_axes(): array = lax.psum(array, axis)  77.4 us
    reshape x5, local copies, waits for them, and re-layouts, blocks(): return field.reshape(a // 2, 2, b // 2, 2, c // 2, 2)  60.8 us
    ppermute x63, waiting for transfers between devices, extended(): lax.ppermute(tail, axis, [(i, (i + 1) % count) for i in range(ends)])  58.3 us
    all_gather x2, blocking collectives, one_gather(): lines, at, outs = (lax.all_gather(line, axis), 0, [])  50.3 us
    reshape x4, local copies, waits for them, and re-layouts, prolong(): return wide.reshape(2 * a, 2 * b, 2 * c)  30.8 us
  transfers between devices with their start and end apart: 126, of which 75 were waited for; matrix products, arithmetic and copies ran while one was open for 4% of the time, Pallas kernels for 0%

commit v1 on v0

--- a/solution.py
+++ b/solution.py
@@ -7,6 +7,12 @@
 ITERS = 2
 GX_GY_GZ = ("gx", "gy_0", "gy_1", "gz")
 GY = ("gy_0", "gy_1")
+
+
+def summed_here(x, name):
+    terms = lax.all_gather(x, name, axis=0, tiled=False)
+    summed = terms.sum(axis=0)
+    return summed
 
 
 def extended(cells, sides, width):
@@ -44,7 +50,7 @@
 
 def over_axes(array, axes):
     for axis in axes:
-        array = lax.psum(array, axis)
+        array = summed_here(array, axis)
     return array
 
 

time: 859 us -> 902 us (1.050)
  local copies, waits for them, and re-layouts: 118 us -> 154 us
  other arithmetic: 47 us -> 61.8 us
    psum x8 -> x0, blocking collectives: 77.4 us -> none  [over_axes(): array = lax.psum(array, axis)]
    unnamed x0 -> x8, blocking collectives: none -> 71.9 us
    unnamed x36 -> x94, local copies, waits for them, and re-layouts: 2.01 us -> 38 us
    reduce_sum x0 -> x24, other arithmetic: none -> 14.7 us  [summed_here(): summed = terms.sum(axis=0)]
  transfers between devices with their start and end apart: 126 -> 126, of which waited for: 75 -> 74; matrix products, arithmetic and copies ran while one was open for 4% -> 3% of each run, Pallas kernels for 0% -> 0%
where the time goes in v1:
time: 902 us; the launch traced here: 890 us
  starting transfers between devices  304 us (34%)
  waiting for transfers between devices  239 us (26%)
  local copies, waits for them, and re-layouts  154 us (17%)
  blocking collectives  122 us (14%)
  other arithmetic  61.8 us (7%)
  between operations  9.04 us (1%)
    ppermute x63, waiting for transfers between devices, extended(): lax.ppermute(head, axis, [((i + 1) % count, i) for i in range(ends)])  184 us
    ppermute x63, starting transfers between devices, extended(): lax.ppermute(tail, axis, [(i, (i + 1) % count) for i in range(ends)])  168 us
    ppermute x63, starting transfers between devices, extended(): lax.ppermute(head, axis, [((i + 1) % count, i) for i in range(ends)])  136 us
    unnamed x8, blocking collectives  71.9 us
    reshape x5, local copies, waits for them, and re-layouts, blocks(): return field.reshape(a // 2, 2, b // 2, 2, c // 2, 2)  60.7 us
    ppermute x63, waiting for transfers between devices, extended(): lax.ppermute(tail, axis, [(i, (i + 1) % count) for i in range(ends)])  54.7 us
    all_gather x2, blocking collectives, one_gather(): lines, at, outs = (lax.all_gather(line, axis), 0, [])  50.1 us
    unnamed x94, local copies, waits for them, and re-layouts  38 us
  transfers between devices with their start and end apart: 126, of which 74 were waited for; matrix products, arithmetic and copies ran while one was open for 3% of the time, Pallas kernels for 0%

profile of v1, /device:TPU:2, one launch (start us, length us, event | category | flops | bytes accessed | tf_op | source)
XLA Modules:
  0.0 889.6 jit_solution(1407139920446362880)
XLA Ops:
  52.7 18.1 %reshape.156 = f32[8,2,16,2,64,2]{5,4,3,2,1,0:T(8,128)} reshape(f32[16,32,128]{2,1,0:T(8,128)S(1)} %fusion.32) | data formatting | bytes 524288 | tf_op jit(solution)/shard_map/reshape | solution.py:98
  70.8 7.0 reduce_sum.374
  100.9 18.1 %reshape.157 = f32[8,2,16,2,64,2]{5,4,3,2,1,0:T(8,128)} reshape(f32[16,32,128]{2,1,0:T(8,128)S(1)} %copy-done) | data formatting | bytes 524288 | tf_op jit(solution)/shard_map/reshape | solution.py:98
  118.9 7.0 reduce_sum.375
  166.8 25.5 %all-gather = f32[16384]{0:T(1024)S(1)} all-gather(f32[2048]{0:T(1024)S(1)} %pad_maximum_fusion.41), channel_id=2, replica_groups=mesh['gx'=4,'gy_0'=4,'gy_1'=2,'gz'=8] {'gz'}, dimensions={0}, use_global_device_ids=true | all-gather | bytes 73728 | tf_op jit(solution)/shard_map/all_gather | solution.py:43
  293.3 6.5 broadcast_in_dim.11
  299.8 12.6 %reshape.162 = f32[16,32,128]{2,1,0:T(8,128)S(1)} reshape(f32[8,2,16,2,64,2]{5,4,3,2,1,0:T(8,128)} %broadcast_in_dim.11) | data formatting | bytes 524288 | tf_op jit(solution)/shard_map/reshape | solution.py:108
  332.2 6.1 collective-permute-done.52
  363.3 6.1 collective-permute-done.58
  411.7 9.7 %all-reduce.35 = (f32[4]{0:T(128)S(1)}, f32[4]{0:T(128)S(1)}, f32[4]{0:T(128)S(1)}) all-reduce(f32[4]{0:T(128)S(1)} %dynamic-update-slice, f32[4]{0:T(128)S(1)} %dynamic-update-slice.4, f32[4]{0:T(128)S(1)} %dynamic-update-slice.8), channel_id=1, replica_groups=mesh['gx'=4,'gy_0'=4,'gy_1'=2,'gz'=8] {'gx'}, use_global_device_ids=true, to_apply=%add.6 | all-reduce | flops 12 | bytes 96
  428.1 8.2 all-reduce.33
  451.6 15.6 %all-reduce.31 = (f32[8]{0:T(128)S(1)}, f32[8]{0:T(128)S(1)}, f32[8]{0:T(128)S(1)}) all-reduce(f32[8]{0:T(128)S(1)} %dynamic-update-slice.3, f32[8]{0:T(128)S(1)} %dynamic-update-slice.7, f32[8]{0:T(128)S(1)} %dynamic-update-slice.11), channel_id=1, replica_groups=mesh['gx'=4,'gy_0'=4,'gy_1'=2,'gz'=8] {'gz'}, use_global_device_ids=true, to_apply=%add.9 | all-reduce | flops 24 | bytes 192
  489.0 6.9 collective-permute-done.70
  504.4 18.1 %reshape.163 = f32[8,2,16,2,64,2]{5,4,3,2,1,0:T(8,128)} reshape(f32[16,32,128]{2,1,0:T(8,128)S(1)} %fusion.21) | data formatting | bytes 524288 | tf_op jit(solution)/shard_map/reshape | solution.py:98
  522.5 7.0 reduce_sum.397
  589.2 24.6 %all-gather.1 = f32[16384]{0:T(1024)S(1)} all-gather(f32[2048]{0:T(1024)S(1)} %pad_maximum_fusion.40), channel_id=3, replica_groups=mesh['gx'=4,'gy_0'=4,'gy_1'=2,'gz'=8] {'gz'}, dimensions={0}, use_global_device_ids=true | all-gather | bytes 73728 | tf_op jit(solution)/shard_map/all_gather | solution.py:43
  712.5 6.5 broadcast_in_dim.14
  719.0 12.6 %reshape.168 = f32[16,32,128]{2,1,0:T(8,128)S(1)} reshape(f32[8,2,16,2,64,2]{5,4,3,2,1,0:T(8,128)} %broadcast_in_dim.14) | data formatting | bytes 524288 | tf_op jit(solution)/shard_map/reshape | solution.py:108
  751.8 6.1 collective-permute-done.112
  783.3 6.0 collective-permute-done.118
  812.9 6.1 collective-permute-done.124
  829.4 9.7 %all-reduce.34 = (f32[4]{0:T(128)S(1)}, f32[4]{0:T(128)S(1)}, f32[4]{0:T(128)S(1)}) all-reduce(f32[4]{0:T(128)S(1)} %dynamic-update-slice.12, f32[4]{0:T(128)S(1)} %dynamic-update-slice.16, f32[4]{0:T(128)S(1)} %dynamic-update-slice.20), channel_id=1, replica_groups=mesh['gx'=4,'gy_0'=4,'gy_1'=2,'gz'=8] {'gx'}, use_global_device_ids=true, to_apply=%add.18 | all-reduce | flops 12 | bytes 96
  845.1 8.2 all-reduce.32
  867.7 15.6 %all-reduce.30 = (f32[8]{0:T(128)S(1)}, f32[8]{0:T(128)S(1)}, f32[8]{0:T(128)S(1)}) all-reduce(f32[8]{0:T(128)S(1)} %dynamic-update-slice.15, f32[8]{0:T(128)S(1)} %dynamic-update-slice.19, f32[8]{0:T(128)S(1)} %dynamic-update-slice.23), channel_id=1, replica_groups=mesh['gx'=4,'gy_0'=4,'gy_1'=2,'gz'=8] {'gz'}, use_global_device_ids=true, to_apply=%add.21 | all-reduce | flops 24 | bytes 192
  (598 shorter events, 612.4 us)
Async XLA Ops:
  1.5 12.6 %collective-permute-start = (f32[2,32,128]{2,1,0:T(8,128)S(1)}, f32[2,32,128]{2,1,0:T(8,128)S(1)}, u32[]{:S(2)}, u32[]{:S(2)}) collective-permute-start(f32[2,32,128]{2,1,0:T(8,128)S(1)} %get-tuple-element.99), channel_id=1, source_target_pairs={{0,64},{64,128},{128,192},{1,65},{65,129},{129,193},{2,66},{66,130... | collective-permute-start | bytes 98312 | tf_op jit(solution)/shard_map/ppermute | solution.py:26
  4.9 10.2 %collective-permute-start.1 = (f32[2,32,128]{2,1,0:T(8,128)S(1)}, f32[2,32,128]{2,1,0:T(8,128)S(1)}, u32[]{:S(2)}, u32[]{:S(2)}) collective-permute-start(f32[2,32,128]{2,1,0:T(8,128)S(1)} %get-tuple-element.98), channel_id=1, source_target_pairs={{64,0},{128,64},{192,128},{65,1},{129,65},{193,129},{66,2},{130,66... | collective-permute-start | bytes 98312 | tf_op jit(solution)/shard_map/ppermute | solution.py:28
  15.1 9.8 %collective-permute-start.2 = (f32[20,2,128]{2,1,0:T(2,128)S(1)}, f32[20,2,128]{2,1,0:T(2,128)S(1)}, u32[]{:S(2)}, u32[]{:S(2)}) collective-permute-start(f32[20,2,128]{2,1,0:T(2,128)S(1)} %get-tuple-element.68), channel_id=1, source_target_pairs={{0,8},{8,16},{16,24},{24,32},{32,40},{40,48},{48,56},{1,9},{9,17},... | collective-permute-start | bytes 61448 | tf_op jit(solution)/shard_map/ppermute | solution.py:26
  18.8 11.6 %collective-permute-start.8 = (f32[20,2,128]{2,1,0:T(2,128)S(1)}, f32[20,2,128]{2,1,0:T(2,128)S(1)}, u32[]{:S(2)}, u32[]{:S(2)}) collective-permute-start(f32[20,2,128]{2,1,0:T(2,128)S(1)} %get-tuple-element.66), channel_id=1, source_target_pairs={{0,8},{8,16},{16,24},{24,32},{32,40},{40,48},{48,56},{1,9},{9,17},... | collective-permute-start | bytes 61448 | tf_op jit(solution)/shard_map/ppermute | solution.py:26
  25.2 12.2 %collective-permute-start.4 = (f32[20,36,2]{2,1,0:T(8,128)S(1)}, f32[20,36,2]{2,1,0:T(8,128)S(1)}, u32[]{:S(2)}, u32[]{:S(2)}) collective-permute-start(f32[20,36,2]{2,1,0:T(8,128)S(1)} %get-tuple-element.50), channel_id=1, source_target_pairs={{0,1},{1,2},{2,3},{3,4},{4,5},{5,6},{6,7},{8,9},{9,10},{10,11},{11... | collective-permute-start | bytes 17288 | tf_op jit(solution)/shard_map/ppermute | solution.py:26
  29.1 12.9 %collective-permute-start.5 = (f32[20,36,2]{2,1,0:T(8,128)S(1)}, f32[20,36,2]{2,1,0:T(8,128)S(1)}, u32[]{:S(2)}, u32[]{:S(2)}) collective-permute-start(f32[20,36,2]{2,1,0:T(8,128)S(1)} %get-tuple-element.51), channel_id=1, source_target_pairs={{1,0},{2,1},{3,2},{4,3},{5,4},{6,5},{7,6},{9,8},{10,9},{11,10},{12... | collective-permute-start | bytes 17288 | tf_op jit(solution)/shard_map/ppermute | solution.py:28
  30.7 15.6 %collective-permute-start.10 = (f32[20,36,2]{2,1,0:T(8,128)S(1)}, f32[20,36,2]{2,1,0:T(8,128)S(1)}, u32[]{:S(2)}, u32[]{:S(2)}) collective-permute-start(f32[20,36,2]{2,1,0:T(8,128)S(1)} %get-tuple-element.48), channel_id=1, source_target_pairs={{0,1},{1,2},{2,3},{3,4},{4,5},{5,6},{6,7},{8,9},{9,10},{10,11},{11... | collective-permute-start | bytes 17288 | tf_op jit(solution)/shard_map/ppermute | solution.py:26
  35.2 15.5 %collective-permute-start.11 = (f32[20,36,2]{2,1,0:T(8,128)S(1)}, f32[20,36,2]{2,1,0:T(8,128)S(1)}, u32[]{:S(2)}, u32[]{:S(2)}) collective-permute-start(f32[20,36,2]{2,1,0:T(8,128)S(1)} %get-tuple-element.49), channel_id=1, source_target_pairs={{1,0},{2,1},{3,2},{4,3},{5,4},{6,5},{7,6},{9,8},{10,9},{11,10},{12... | collective-permute-start | bytes 17288 | tf_op jit(solution)/shard_map/ppermute | solution.py:28
  95.7 30.2 %collective-permute-start.16 = (f32[10,18,1]{2,1,0:T(8,128)S(1)}, f32[10,18,1]{2,1,0:T(8,128)S(1)}, u32[]{:S(2)}, u32[]{:S(2)}) collective-permute-start(f32[10,18,1]{2,1,0:T(8,128)S(1)} %get-tuple-element.114), channel_id=1, source_target_pairs={{0,1},{1,2},{2,3},{3,4},{4,5},{5,6},{6,7},{8,9},{9,10},{10,11},{11... | collective-permute-start | bytes 2168 | tf_op jit(solution)/shard_map/ppermute | solution.py:26
  99.6 26.4 %collective-permute-start.17 = (f32[10,18,1]{2,1,0:T(8,128)S(1)}, f32[10,18,1]{2,1,0:T(8,128)S(1)}, u32[]{:S(2)}, u32[]{:S(2)}) collective-permute-start(f32[10,18,1]{2,1,0:T(8,128)S(1)} %get-tuple-element.115), channel_id=1, source_target_pairs={{1,0},{2,1},{3,2},{4,3},{5,4},{6,5},{7,6},{9,8},{10,9},{11,10},{12... | collective-permute-start | bytes 2168 | tf_op jit(solution)/shard_map/ppermute | solution.py:28
  327.2 11.1 %collective-permute-start.52 = (f32[18,34,1]{2,1,0:T(8,128)S(1)}, f32[18,34,1]{2,1,0:T(8,128)S(1)}, u32[]{:S(2)}, u32[]{:S(2)}) collective-permute-start(f32[18,34,1]{2,1,0:T(8,128)S(1)} %get-tuple-element.62), channel_id=1, source_target_pairs={{0,1},{1,2},{2,3},{3,4},{4,5},{5,6},{6,7},{8,9},{9,10},{10,11},{11... | collective-permute-start | bytes 7352 | tf_op jit(solution)/shard_map/ppermute | solution.py:26
  330.9 12.2 %collective-permute-start.53 = (f32[18,34,1]{2,1,0:T(8,128)S(1)}, f32[18,34,1]{2,1,0:T(8,128)S(1)}, u32[]{:S(2)}, u32[]{:S(2)}) collective-permute-start(f32[18,34,1]{2,1,0:T(8,128)S(1)} %get-tuple-element.63), channel_id=1, source_target_pairs={{1,0},{2,1},{3,2},{4,3},{5,4},{6,5},{7,6},{9,8},{10,9},{11,10},{12... | collective-permute-start | bytes 7352 | tf_op jit(solution)/shard_map/ppermute | solution.py:28
  358.6 10.9 %collective-permute-start.58 = (f32[18,34,1]{2,1,0:T(8,128)S(1)}, f32[18,34,1]{2,1,0:T(8,128)S(1)}, u32[]{:S(2)}, u32[]{:S(2)}) collective-permute-start(f32[18,34,1]{2,1,0:T(8,128)S(1)} %get-tuple-element.60), channel_id=1, source_target_pairs={{0,1},{1,2},{2,3},{3,4},{4,5},{5,6},{6,7},{8,9},{9,10},{10,11},{11... | collective-permute-start | bytes 7352 | tf_op jit(solution)/shard_map/ppermute | solution.py:26
  362.0 12.2 %collective-permute-start.59 = (f32[18,34,1]{2,1,0:T(8,128)S(1)}, f32[18,34,1]{2,1,0:T(8,128)S(1)}, u32[]{:S(2)}, u32[]{:S(2)}) collective-permute-start(f32[18,34,1]{2,1,0:T(8,128)S(1)} %get-tuple-element.61), channel_id=1, source_target_pairs={{1,0},{2,1},{3,2},{4,3},{5,4},{6,5},{7,6},{9,8},{10,9},{11,10},{12... | collective-permute-start | bytes 7352 | tf_op jit(solution)/shard_map/ppermute | solution.py:28
  389.6 11.1 %collective-permute-start.64 = (f32[18,34,1]{2,1,0:T(8,128)S(1)}, f32[18,34,1]{2,1,0:T(8,128)S(1)}, u32[]{:S(2)}, u32[]{:S(2)}) collective-permute-start(f32[18,34,1]{2,1,0:T(8,128)S(1)} %get-tuple-element.58), channel_id=1, source_target_pairs={{0,1},{1,2},{2,3},{3,4},{4,5},{5,6},{6,7},{8,9},{9,10},{10,11},{11... | collective-permute-start | bytes 7352 | tf_op jit(solution)/shard_map/ppermute | solution.py:26
  393.3 12.2 %collective-permute-start.65 = (f32[18,34,1]{2,1,0:T(8,128)S(1)}, f32[18,34,1]{2,1,0:T(8,128)S(1)}, u32[]{:S(2)}, u32[]{:S(2)}) collective-permute-start(f32[18,34,1]{2,1,0:T(8,128)S(1)} %get-tuple-element.59), channel_id=1, source_target_pairs={{1,0},{2,1},{3,2},{4,3},{5,4},{6,5},{7,6},{9,8},{10,9},{11,10},{12... | collective-permute-start | bytes 7352 | tf_op jit(solution)/shard_map/ppermute | solution.py:28
  485.2 10.7 %collective-permute-start.70 = (f32[20,36,2]{2,1,0:T(8,128)S(1)}, f32[20,36,2]{2,1,0:T(8,128)S(1)}, u32[]{:S(2)}, u32[]{:S(2)}) collective-permute-start(f32[20,36,2]{2,1,0:T(8,128)S(1)} %get-tuple-element.46), channel_id=1, source_target_pairs={{0,1},{1,2},{2,3},{3,4},{4,5},{5,6},{6,7},{8,9},{9,10},{10,11},{11... | collective-permute-start | bytes 17288 | tf_op jit(solution)/shard_map/ppermute | solution.py:26
  487.7 12.9 %collective-permute-start.71 = (f32[20,36,2]{2,1,0:T(8,128)S(1)}, f32[20,36,2]{2,1,0:T(8,128)S(1)}, u32[]{:S(2)}, u32[]{:S(2)}) collective-permute-start(f32[20,36,2]{2,1,0:T(8,128)S(1)} %get-tuple-element.47), channel_id=1, source_target_pairs={{1,0},{2,1},{3,2},{4,3},{5,4},{6,5},{7,6},{9,8},{10,9},{11,10},{12... | collective-permute-start | bytes 17288 | tf_op jit(solution)/shard_map/ppermute | solution.py:28
  746.6 11.4 %collective-permute-start.112 = (f32[18,34,1]{2,1,0:T(8,128)S(1)}, f32[18,34,1]{2,1,0:T(8,128)S(1)}, u32[]{:S(2)}, u32[]{:S(2)}) collective-permute-start(f32[18,34,1]{2,1,0:T(8,128)S(1)} %get-tuple-element.56), channel_id=1, source_target_pairs={{0,1},{1,2},{2,3},{3,4},{4,5},{5,6},{6,7},{8,9},{9,10},{10,11},{11... | collective-permute-start | bytes 7352 | tf_op jit(solution)/shard_map/ppermute | solution.py:26
  750.5 11.9 %collective-permute-start.113 = (f32[18,34,1]{2,1,0:T(8,128)S(1)}, f32[18,34,1]{2,1,0:T(8,128)S(1)}, u32[]{:S(2)}, u32[]{:S(2)}) collective-permute-start(f32[18,34,1]{2,1,0:T(8,128)S(1)} %get-tuple-element.57), channel_id=1, source_target_pairs={{1,0},{2,1},{3,2},{4,3},{5,4},{6,5},{7,6},{9,8},{10,9},{11,10},{12... | collective-permute-start | bytes 7352 | tf_op jit(solution)/shard_map/ppermute | solution.py:28
  778.1 11.1 %collective-permute-start.118 = (f32[18,34,1]{2,1,0:T(8,128)S(1)}, f32[18,34,1]{2,1,0:T(8,128)S(1)}, u32[]{:S(2)}, u32[]{:S(2)}) collective-permute-start(f32[18,34,1]{2,1,0:T(8,128)S(1)} %get-tuple-element.54), channel_id=1, source_target_pairs={{0,1},{1,2},{2,3},{3,4},{4,5},{5,6},{6,7},{8,9},{9,10},{10,11},{11... | collective-permute-start | bytes 7352 | tf_op jit(solution)/shard_map/ppermute | solution.py:26
  781.8 12.2 %collective-permute-start.119 = (f32[18,34,1]{2,1,0:T(8,128)S(1)}, f32[18,34,1]{2,1,0:T(8,128)S(1)}, u32[]{:S(2)}, u32[]{:S(2)}) collective-permute-start(f32[18,34,1]{2,1,0:T(8,128)S(1)} %get-tuple-element.55), channel_id=1, source_target_pairs={{1,0},{2,1},{3,2},{4,3},{5,4},{6,5},{7,6},{9,8},{10,9},{11,10},{12... | collective-permute-start | bytes 7352 | tf_op jit(solution)/shard_map/ppermute | solution.py:28
  808.4 10.6 %collective-permute-start.124 = (f32[18,34,1]{2,1,0:T(8,128)S(1)}, f32[18,34,1]{2,1,0:T(8,128)S(1)}, u32[]{:S(2)}, u32[]{:S(2)}) collective-permute-start(f32[18,34,1]{2,1,0:T(8,128)S(1)} %get-tuple-element.52), channel_id=1, source_target_pairs={{0,1},{1,2},{2,3},{3,4},{4,5},{5,6},{6,7},{8,9},{9,10},{10,11},{11... | collective-permute-start | bytes 7352 | tf_op jit(solution)/shard_map/ppermute | solution.py:26
  811.6 12.2 %collective-permute-start.125 = (f32[18,34,1]{2,1,0:T(8,128)S(1)}, f32[18,34,1]{2,1,0:T(8,128)S(1)}, u32[]{:S(2)}, u32[]{:S(2)}) collective-permute-start(f32[18,34,1]{2,1,0:T(8,128)S(1)} %get-tuple-element.53), channel_id=1, source_target_pairs={{1,0},{2,1},{3,2},{4,3},{5,4},{6,5},{7,6},{9,8},{10,9},{11,10},{12... | collective-permute-start | bytes 7352 | tf_op jit(solution)/shard_map/ppermute | solution.py:28
  (121 other events, 2157.8 us)
